TPU v7x, 32 devices: a whole 2x2x4 slice. The times are simulated.
32 devices in a mesh: vec: 4 (over y, x), orb: 8 (over z, core).
Axes of the slice: x: 2, y: 2, z: 4, core: 2. Of those that a mesh axis runs over, the one named last changes fastest.
Arguments:
- chol_occ: float32 [44, 96, 1056], P('vec', 'orb'), may hold values from -6 to 6
- chol_vir: float32 [44, 960, 1056], P('vec', 'orb'), may hold values from -6 to 6
- singles: float32 [96, 960], P('orb'), may hold values from -0.6 to 0.6
Outputs:
- dressed_vir: float32 [44, 960, 1056], P('vec', 'orb')
- dressed_ov: float32 [44, 96, 960], P(None, 'orb', 'vec')
- fock_ov: float32 [96, 960], P('orb')
All inputs are finite; a program needn't handle non-finite values.
Results may differ from a plain program's by a relative error of at most 0.000086.
Values sent between devices are 32-bit elements; how exact they have to be, the bound alone decides.
A program may use at most 64 MiB of HBM per device.

v0:
```python
import jax
import jax.numpy as jnp
from jax import lax
from jax.experimental import pallas as pl
from jax.experimental.pallas import tpu as pltpu
from jax.sharding import PartitionSpec as P

MESH = pl.DeviceIdType.MESH
F32, BF16 = jnp.float32, jnp.bfloat16
LANES = 128
CORES = 2
SKEW = 1
AHEAD = 4


def split(x):
    hi = x.astype(BF16)
    return hi, (x - hi.astype(F32)).astype(BF16)


def dot(a, b):
    return jnp.dot(a, b, preferred_element_type=F32)


def make_kernel(W, D, Q, R, RV, N, A):
    OCC = N - A
    NZ = D // CORES
    GR = 8 if R % 8 == 0 else (4 if R % 4 == 0 else R)
    NJ = R // GR
    ROWS = Q * R
    GRAN = Q * NJ
    MAIN = N // LANES * LANES
    TAIL = N - MAIN
    SLOTS = LANES // TAIL if TAIL else 1
    GROUPS = -(-Q // SLOTS)
    PIECE = A // W
    KP = -(-OCC // LANES) * LANES
    UNITS = Q + 2
    NP = -(-N // LANES) * LANES
    AP = -(-A // LANES) * LANES
    VP = -(-RV // LANES) * LANES

    def kernel(occ, vir, sing, out_vir, out_ov, out_fock,
               gath, amps, tails, vloc, oloc, sloc, xbuf, drows, tmat, tright, sleft, lwts,
               ovsend, ovrecv, ovout, fbuf, fout,
               s_right, s_left, s_part, r_sem, ov_s, ov_r, f_s, f_r, in_sem, v_in, v_out, o_out):
        v = lax.axis_index("vec")
        o = lax.axis_index("orb")
        z = o // CORES
        k = o % CORES
        has_r = z < NZ - 1
        has_l = z > 0
        right = lax.rem(o + CORES, D)
        left = lax.rem(o - CORES + D, D)
        part = z * CORES + (1 - k)

        c_occ = pltpu.make_async_copy(occ, oloc, in_sem.at[0])
        c_sing = pltpu.make_async_copy(sing, sloc, in_sem.at[1])
        c_occ.start()
        c_sing.start()

        def vin(q):
            return pltpu.make_async_copy(vir.at[q], vloc.at[q], v_in.at[q])

        def vout(q):
            return pltpu.make_async_copy(vloc.at[q], out_vir.at[q], v_out.at[q])

        bar = pltpu.get_barrier_semaphore()

        @pl.when(has_r)
        def _():
            pl.semaphore_signal(bar, inc=1, device_id=(v, right), device_id_type=MESH)

        @pl.when(has_l)
        def _():
            pl.semaphore_signal(bar, inc=1, device_id=(v, left), device_id_type=MESH)

        pl.semaphore_signal(bar, inc=1, device_id=(v, part), device_id_type=MESH)
        for h in range(1, W):
            pl.semaphore_signal(bar, inc=1, device_id=(lax.rem(v + h, W), o), device_id_type=MESH)

        c_occ.wait()
        c_sing.wait()
        for j in range(NJ):
            amps[o, j] = sloc[j * GR:(j + 1) * GR, :]
        for q in range(Q):
            for j in range(NJ):
                gath[o, q * NJ + j] = oloc[q, j * GR:(j + 1) * GR, 0:MAIN]
        if TAIL:
            for g in range(GROUPS):
                parts = [oloc[min(g * SLOTS + t, Q - 1), :, MAIN:N] for t in range(SLOTS)]
                packed = jnp.concatenate(parts, axis=1) if SLOTS > 1 else parts[0]
                for j in range(NJ):
                    tails[o, g * NJ + j, :, 0:SLOTS * TAIL] = packed[j * GR:(j + 1) * GR]
        ri = lax.broadcasted_iota(jnp.int32, (R, KP), 0) + o * R
        ci = lax.broadcasted_iota(jnp.int32, (R, KP), 1)
        mask = ri == ci
        lane = lax.broadcasted_iota(jnp.int32, (GR, LANES), 1)
        tr = jnp.zeros((GR, LANES), F32)
        for q in range(Q):
            dq = jnp.sum(jnp.where(mask, oloc[q, :, 0:KP], 0.0), axis=0, keepdims=True)
            tq = jnp.sum(dq, axis=1, keepdims=True)
            tr = tr + jnp.where(lane == q, jnp.broadcast_to(tq, (GR, LANES)), 0.0)
        tails[o, GROUPS * NJ] = tr

        pl.semaphore_wait(bar, has_r.astype(jnp.int32) + has_l.astype(jnp.int32) + W)

        def piece(d, u):
            if isinstance(u, str):
                return {"a": amps, "t": tails}[u].at[d], {"a": Q, "t": Q + 1}[u]
            return gath.at[d, pl.ds(u * NJ, NJ)], u

        def remote(d, u, sems, target):
            ref, i = piece(d, u)
            return pltpu.make_async_remote_copy(
                src_ref=ref, dst_ref=ref, send_sem=sems.at[d, i], recv_sem=r_sem.at[d, i],
                device_id=(v, target), device_id_type=MESH)

        def send_own(u):
            @pl.when(has_r)
            def _():
                remote(o, u, s_right, right).start()

            @pl.when(has_l)
            def _():
                remote(o, u, s_left, left).start()

            remote(o, u, s_part, part).start()

        def relay(h, u):
            @pl.when(z - h >= 0)
            def _():
                d = (z - h) * CORES + k
                remote(d, u, s_right, right).wait_recv()

                @pl.when(has_r)
                def _():
                    remote(d, u, s_right, right).start()

                remote(d, u, s_part, part).start()

            @pl.when(z + h < NZ)
            def _():
                d = (z + h) * CORES + k
                remote(d, u, s_left, left).wait_recv()

                @pl.when(has_l)
                def _():
                    remote(d, u, s_left, left).start()

                remote(d, u, s_part, part).start()

        def from_partner(u):
            for s in range(NZ):
                remote(s * CORES + 1 - k, u, s_part, part).wait_recv()

        units = ["a", "t"] + list(range(Q))
        LEAD = 2 + SKEW * max(NZ - 2, 0)

        def finish(u):
            for s in range(NZ):
                d = s * CORES + k

                @pl.when(jnp.logical_and(s <= z, has_r))
                def _():
                    remote(d, u, s_right, right).wait_send()

                @pl.when(jnp.logical_and(s >= z, has_l))
                def _():
                    remote(d, u, s_left, left).wait_send()

                remote(d, u, s_part, part).wait_send()

        for u in units[:AHEAD]:
            send_own(u)

        @pl.loop(0, Q)
        def _(q):
            vin(q).start()

        for q in range(Q):
            for r in range(R):
                drows[r * Q + q:r * Q + q + 1, :] = oloc[q, r:r + 1, :]

        for t in range(LEAD):
            if AHEAD <= t + AHEAD < UNITS:
                send_own(units[t + AHEAD])
            for h in range(1, NZ):
                n = t - SKEW * (h - 1)
                if 0 <= n < UNITS:
                    relay(h, units[n])
        from_partner("a")
        from_partner("t")

        xbuf[...] = jnp.zeros_like(xbuf)
        for d in range(D):
            for j in range(NJ):
                at = d * R + j * GR
                xbuf[at:at + GR, 0:A] = amps[d, j]
        amp = xbuf[0:OCC, 0:A]
        tmat[...] = jnp.zeros_like(tmat)
        shifted = jnp.concatenate([jnp.zeros((OCC, OCC), F32), amp], axis=1)
        thi, tlo = split(shifted)
        tmat[0:OCC, :] = thi
        tmat[KP:KP + OCC, :] = tlo
        thi, tlo = split(jnp.transpose(xbuf[:, 0:AP])[0:A])
        tright[:, 0:KP] = thi
        tright[:, KP:2 * KP] = tlo
        ahi, alo = split(xbuf[:, 0:A])
        pick = (lax.broadcasted_iota(jnp.int32, (A, VP), 0)
                == lax.broadcasted_iota(jnp.int32, (A, VP), 1) + o * RV)
        pick = jnp.where(pick, 1.0, 0.0).astype(BF16)
        shi = dot(ahi, pick).astype(BF16)
        sleft[0:KP, 0:VP] = shi
        sleft[KP:2 * KP, 0:VP] = shi
        sleft[0:KP, VP:2 * VP] = dot(alo, pick).astype(BF16)
        sleft[KP:2 * KP, VP:2 * VP] = jnp.zeros((KP, VP), BF16)
        lwts[...] = jnp.zeros_like(lwts)

        keep = lax.broadcasted_iota(jnp.int32, (ROWS, KP), 1) < OCC
        hi, lo = split(jnp.where(keep, drows[:, 0:KP], 0.0))
        extra = dot(jnp.concatenate([hi, hi], axis=1), tmat[...]) + dot(lo, tmat[0:KP, :])
        drows[...] = drows[...] + extra
        for w in range(W):
            sl = drows[:, OCC + w * PIECE:OCC + (w + 1) * PIECE]
            for r in range(R):
                ovsend[w, r] = sl[r * Q:(r + 1) * Q]
        total = tails[0, GROUPS * NJ]
        for d in range(1, D):
            total = total + tails[d, GROUPS * NJ]
        rid = lax.broadcasted_iota(jnp.int32, (R, ROWS), 0) * Q
        cid = lax.broadcasted_iota(jnp.int32, (R, ROWS), 1)
        wts = jnp.zeros((R, ROWS), F32)
        for q in range(Q):
            wts = wts + jnp.where(cid == rid + q, jnp.broadcast_to(total[0:1, q:q + 1], (R, ROWS)), 0.0)
        whi, wlo = split(wts)
        dhi, dlo = split(drows[...])
        fock = (dot(whi, dhi) + (dot(whi, dlo) + dot(wlo, dhi)))[:, OCC:]
        for j in range(NJ):
            fbuf[v, j] = fock[j * GR:(j + 1) * GR]

        def ov_copy(h):
            w = lax.rem(v + h, W)
            return pltpu.make_async_remote_copy(
                src_ref=ovsend.at[w], dst_ref=ovrecv.at[v], send_sem=ov_s.at[h],
                recv_sem=ov_r.at[h], device_id=(w, o), device_id_type=MESH)

        def f_copy(h):
            w = lax.rem(v + h, W)
            return pltpu.make_async_remote_copy(
                src_ref=fbuf.at[v], dst_ref=fbuf.at[v], send_sem=f_s.at[h],
                recv_sem=f_r.at[h], device_id=(w, o), device_id_type=MESH)

        for h in range(1, W):
            ov_copy(h).start()
            f_copy(h).start()
        ovrecv[v] = ovsend[v]

        @pl.loop(0, Q)
        def _(q):
            @pl.when(q + LEAD + AHEAD < UNITS)
            def _():
                send_own(q + LEAD + AHEAD - 2)

            for h in range(1, NZ):
                n = q + LEAD - SKEW * (h - 1)

                @pl.when(n < UNITS)
                def _():
                    relay(h, n - 2)

            from_partner(q)
            if TAIL:
                shift = lax.rem(LANES - lax.rem(q, SLOTS) * TAIL, LANES)
            for d in range(D):
                for j in range(NJ):
                    at = d * R + j * GR
                    xbuf[at:at + GR, 0:MAIN] = gath[d, q * NJ + j]
                    if TAIL:
                        t = pltpu.roll(tails[d, (q // SLOTS) * NJ + j], shift, axis=1)
                        xbuf[at:at + GR, MAIN:N] = t[:, 0:TAIL]
            hi, lo = split(jnp.transpose(xbuf[...])[0:N])
            prod = dot(jnp.concatenate([hi, lo], axis=1), sleft[...])
            prod = prod[:, 0:VP] + prod[:, VP:2 * VP]
            vin(q).wait()
            vloc[q] = vloc[q] - prod[:, 0:RV]
            hi, lo = split(vloc[q, 0:OCC, :])
            lwts[0:OCC, 0:RV] = hi
            lwts[KP:KP + OCC, 0:RV] = hi
            lwts[0:OCC, VP:VP + RV] = lo
            prod = dot(tright[...], lwts[...])
            prod = prod[:, 0:VP] + prod[:, VP:2 * VP]
            vloc[q, OCC:N, :] = vloc[q, OCC:N, :] + prod[:, 0:RV]
            vout(q).start()

        for h in range(1, W):
            ov_copy(h).wait_recv()
            f_copy(h).wait_recv()
        for w in range(W):
            for r in range(R):
                ovout[r, w * Q:(w + 1) * Q, :] = ovrecv[w, r]
        c_ov = pltpu.make_async_copy(ovout, out_ov, o_out.at[0])
        c_ov.start()
        for j in range(NJ):
            acc = fbuf[0, j]
            for w in range(1, W):
                acc = acc + fbuf[w, j]
            fout[j * GR:(j + 1) * GR, :] = acc / (Q * W)
        c_f = pltpu.make_async_copy(fout, out_fock, o_out.at[1])
        c_f.start()

        finish("a")
        finish("t")

        @pl.loop(0, Q)
        def _(u):
            finish(u)
            vout(u).wait()

        for h in range(1, W):
            ov_copy(h).wait_send()
            f_copy(h).wait_send()
        c_ov.wait()
        c_f.wait()

    DMA = pltpu.SemaphoreType.DMA
    V = pltpu.VMEM
    any_spec = pl.BlockSpec(memory_space=pl.ANY)
    return pl.pallas_call(
        kernel,
        name="dress",
        out_shape=(jax.ShapeDtypeStruct((Q, N, RV), F32),
                   jax.ShapeDtypeStruct((R, Q * W, PIECE), F32),
                   jax.ShapeDtypeStruct((R, A), F32)),
        in_specs=[pl.BlockSpec(memory_space=pltpu.HBM)] * 3,
        out_specs=(any_spec,) * 3,
        scratch_shapes=[
            V((D, GRAN, GR, MAIN), F32),
            V((D, NJ, GR, A), F32),
            V((D, GROUPS * NJ + 1, GR, LANES), F32),
            V((Q, N, RV), F32),
            V((Q, R, N), F32),
            V((R, A), F32),
            V((KP, NP), F32),
            V((ROWS, N), F32),
            V((2 * KP, N), BF16),
            V((A, 2 * KP), BF16),
            V((2 * KP, 2 * VP), BF16),
            V((2 * KP, 2 * VP), BF16),
            V((W, R, Q, PIECE), F32),
            V((W, R, Q, PIECE), F32),
            V((R, Q * W, PIECE), F32),
            V((W, NJ, GR, A), F32),
            V((R, A), F32),
            DMA((D, UNITS)), DMA((D, UNITS)), DMA((D, UNITS)), DMA((D, UNITS)),
            DMA((W,)), DMA((W,)), DMA((W,)), DMA((W,)),
            DMA((2,)), DMA((Q,)), DMA((Q,)), DMA((2,)),
        ],
        compiler_params=pltpu.CompilerParams(
            collective_id=0, has_side_effects=True, vmem_limit_bytes=40 * 2**20),
    )


def write_out(*refs):
    n = (len(refs) - 1) // 2
    copies = [pltpu.make_async_copy(refs[i], refs[n + i], refs[-1].at[i]) for i in range(n)]
    for c in copies:
        c.start()
    for c in copies:
        c.wait()


def store(arrays):
    return pl.pallas_call(
        write_out,
        name="store",
        out_shape=tuple(jax.ShapeDtypeStruct(a.shape, a.dtype) for a in arrays),
        in_specs=[pl.BlockSpec(memory_space=pl.ANY)] * len(arrays),
        out_specs=(pl.BlockSpec(memory_space=pltpu.HBM),) * len(arrays),
        scratch_shapes=[pltpu.SemaphoreType.DMA((len(arrays),))],
        compiler_params=pltpu.CompilerParams(vmem_limit_bytes=2**20),
    )(*arrays)


def solution(mesh):
    W, D = mesh.shape["vec"], mesh.shape["orb"]

    def shards(chol_occ, chol_vir, singles):
        Q, R, N = chol_occ.shape
        call = make_kernel(W, D, Q, R, chol_vir.shape[1], N, singles.shape[1])
        args = (chol_occ, jnp.swapaxes(chol_vir, 1, 2), singles)
        vir, ov, fock = store(call(*(pltpu.with_memory_space_constraint(a, pltpu.HBM) for a in args)))
        return jnp.swapaxes(vir, 1, 2), jnp.swapaxes(ov, 0, 1), fock

    return jax.shard_map(
        shards,
        mesh=mesh,
        in_specs=(P("vec", "orb", None), P("vec", "orb", None), P("orb", None)),
        out_specs=(P("vec", "orb", None), P(None, "orb", "vec"), P("orb", None)),
        check_vma=False,
    )
```

profile of v0, /device:TPU:0, one launch (start us, length us, event | category | flops | bytes accessed | tf_op | source)
XLA Modules:
  0.0 57.5 jit_solution(17905803165476238225)
XLA Ops:
  0.6 54.1 %dress.1 = (f32[11,1056,120]{2,1,0:T(8,128)S(1)}, f32[12,44,240]{2,1,0:T(8,128)S(1)}, f32[12,960]{1,0:T(8,128)S(1)}) custom-call(f32[11,12,1056]{2,1,0:T(8,128)} %occ.1, f32[11,1056,120]{2,1,0:T(8,128)} %bitcast.3, f32[12,960]{1,0:T(8,128)} %sing.1), custom_call_target="tpu_custom_call" | custom-call | tf_op jit(solution)/shard_map/dress/pallas_call | solution.py:392
  54.7 2.8 %store.1 = (f32[11,1056,120]{2,1,0:T(8,128)}, f32[12,44,240]{2,1,0:T(8,128)}, f32[12,960]{1,0:T(8,128)}) custom-call(f32[11,1056,120]{2,1,0:T(8,128)S(1)} %get-tuple-element.9.refs_0_, f32[12,44,240]{2,1,0:T(8,128)S(1)} %get-tuple-element.10.refs_1_, f32[12,960]{1,0:T(8,128)S(1)} %get-tuple-element.11.refs_2_), custom_call_target="tpu_custom_call" | custom-call | tf_op jit(solution)/shard_map/store/pallas_call | solution.py:374
where the time goes:
time: 57.7 us; the launch traced here: 57.5 us
  Pallas kernels  56.9 us (99%)
  between operations  0.64 us (1%)
    pallas_call x1, Pallas kernels, shards(): call(*(pltpu.with_memory_space_constraint(a, pltpu.HBM) for a in args))  54.1 us
    pallas_call x1, Pallas kernels, store(): pl.pallas_call(write_out, name='store', out_shape=tuple((jax.ShapeDtypeSt...  2.8 us

commit v1 on v0

--- a/solution.py
+++ b/solution.py
@@ -11,6 +11,8 @@
 CORES = 2
 SKEW = 1
 AHEAD = 4
+FIRST = 5
+RATE = 2
 
 
 def split(x):
@@ -35,15 +37,25 @@
     GROUPS = -(-Q // SLOTS)
     PIECE = A // W
     KP = -(-OCC // LANES) * LANES
-    UNITS = Q + 2
+    UNITS = Q + 1
     NP = -(-N // LANES) * LANES
     AP = -(-A // LANES) * LANES
     VP = -(-RV // LANES) * LANES
+    TILES = AP // LANES
+    CH = -(-TILES // W)
+    NCH = -(-TILES // CH)
+    HT = GROUPS * NJ
+    HS = HT + 1
+    HEAD = HS + NJ * CH
+    LAG = SKEW * max(NZ - 2, 0)
+    STEPS = UNITS + LAG
+    START = max(FIRST, LAG + 1)
 
     def kernel(occ, vir, sing, out_vir, out_ov, out_fock,
-               gath, amps, tails, vloc, oloc, sloc, xbuf, drows, tmat, tright, sleft, lwts,
+               gath, head, amps, vloc, oloc, sloc, xbuf, drows, tmat, tright, sleft, lwts,
                ovsend, ovrecv, ovout, fbuf, fout,
-               s_right, s_left, s_part, r_sem, ov_s, ov_r, f_s, f_r, in_sem, v_in, v_out, o_out):
+               s_right, s_left, s_part, r_dir, r_part, a_s, a_r, ov_s, ov_r, f_s, f_r,
+               in_sem, v_in, v_out, o_out):
         v = lax.axis_index("vec")
         o = lax.axis_index("orb")
         z = o // CORES
@@ -59,11 +71,10 @@
         c_occ.start()
         c_sing.start()
 
-        def vin(q):
-            return pltpu.make_async_copy(vir.at[q], vloc.at[q], v_in.at[q])
+        c_vir = pltpu.make_async_copy(vir, vloc, v_in.at[0])
 
         def vout(q):
-            return pltpu.make_async_copy(vloc.at[q], out_vir.at[q], v_out.at[q])
+            return pltpu.make_async_copy(vloc.at[q], out_vir.at[q], v_out.at[0])
 
         bar = pltpu.get_barrier_semaphore()
 
@@ -79,19 +90,122 @@
         for h in range(1, W):
             pl.semaphore_signal(bar, inc=1, device_id=(lax.rem(v + h, W), o), device_id_type=MESH)
 
+        def piece(c, s, u):
+            if isinstance(u, str):
+                return head.at[c, s], 0, 0
+            return gath.at[c, s, pl.ds(u * NJ, NJ)], u + 1, 1
+
+        def remote(s, u, sems, target):
+            ref, i, kind = piece(k, s, u)
+            return pltpu.make_async_remote_copy(
+                src_ref=ref, dst_ref=ref, send_sem=sems.at[s, kind], recv_sem=r_dir.at[s, i],
+                device_id=(v, target), device_id_type=MESH)
+
+        def across(s, u):
+            ref, i, kind = piece(k, s, u)
+            return pltpu.make_async_remote_copy(
+                src_ref=ref, dst_ref=ref, send_sem=s_part.at[s, kind], recv_sem=r_part.at[i],
+                device_id=(v, part), device_id_type=MESH)
+
+        def send_own(u):
+            @pl.when(has_r)
+            def _():
+                remote(z, u, s_right, right).start()
+
+            @pl.when(has_l)
+            def _():
+                remote(z, u, s_left, left).start()
+
+            across(z, u).start()
+
+        def relay(h, u):
+            @pl.when(z - h >= 0)
+            def _():
+                s = z - h
+                remote(s, u, s_right, right).wait_recv()
+
+                @pl.when(has_r)
+                def _():
+                    remote(s, u, s_right, right).start()
+
+                across(s, u).start()
+
+            @pl.when(z + h < NZ)
+            def _():
+                s = z + h
+                remote(s, u, s_left, left).wait_recv()
+
+                @pl.when(has_l)
+                def _():
+                    remote(s, u, s_left, left).start()
+
+                across(s, u).start()
+
+        def from_partner(u):
+            if isinstance(u, str):
+                ref, i = head.at[1 - k], 0
+            else:
+                ref, i = gath.at[1 - k, :, pl.ds(u * NJ, NJ)], u + 1
+            pltpu.make_async_remote_copy(
+                src_ref=ref, dst_ref=ref, send_sem=s_part.at[0, 0], recv_sem=r_part.at[i],
+                device_id=(v, part), device_id_type=MESH).wait_recv()
+
+        def finish():
+            for s in range(NZ):
+                for kind, ref in enumerate((head.at[k, s], gath.at[k, s])):
+                    def drain(sems, target):
+                        pltpu.make_async_remote_copy(
+                            src_ref=ref, dst_ref=ref, send_sem=sems.at[s, kind], recv_sem=r_dir.at[s, 0],
+                            device_id=(v, target), device_id_type=MESH).wait_send()
+
+                    @pl.when(jnp.logical_and(s <= z, has_r))
+                    def _():
+                        drain(s_right, right)
+
+                    @pl.when(jnp.logical_and(s >= z, has_l))
+                    def _():
+                        drain(s_left, left)
+
+                    drain(s_part, part)
+
+        def a_copy(h):
+            w = lax.rem(v + h, W)
+            c = lax.rem(v, NCH)
+            return pltpu.make_async_remote_copy(
+                src_ref=head.at[:, :, pl.ds(HS, NJ * CH)], dst_ref=amps.at[c], send_sem=a_s.at[h],
+                recv_sem=a_r.at[c], device_id=(w, o), device_id_type=MESH)
+
+        def a_wait(c):
+            @pl.when(c != v)
+            def _():
+                pltpu.make_async_remote_copy(
+                    src_ref=amps.at[c], dst_ref=amps.at[c], send_sem=a_s.at[0],
+                    recv_sem=a_r.at[c], device_id=(lax.rem(v + 1, W), o), device_id_type=MESH).wait_recv()
+
+        def repack(q):
+            for j in range(NJ):
+                gath[k, z, q * NJ + j] = oloc[q, j * GR:(j + 1) * GR, 0:MAIN]
+
+        units = ["h"] + list(range(Q))
         c_occ.wait()
         c_sing.wait()
-        for j in range(NJ):
-            amps[o, j] = sloc[j * GR:(j + 1) * GR, :]
-        for q in range(Q):
+        full = sloc[...]
+        if NCH * CH * LANES > A:
+            full = jnp.concatenate([full, jnp.zeros((R, NCH * CH * LANES - A), F32)], axis=1)
+        mine = lax.rem(v, NCH)
+        for t in range(CH):
+            val = full[:, t * LANES:(t + 1) * LANES]
+            for c in range(1, NCH):
+                at = (c * CH + t) * LANES
+                val = jnp.where(mine == c, full[:, at:at + LANES], val)
             for j in range(NJ):
-                gath[o, q * NJ + j] = oloc[q, j * GR:(j + 1) * GR, 0:MAIN]
+                head[k, z, HS + j * CH + t] = val[j * GR:(j + 1) * GR]
         if TAIL:
             for g in range(GROUPS):
                 parts = [oloc[min(g * SLOTS + t, Q - 1), :, MAIN:N] for t in range(SLOTS)]
                 packed = jnp.concatenate(parts, axis=1) if SLOTS > 1 else parts[0]
                 for j in range(NJ):
-                    tails[o, g * NJ + j, :, 0:SLOTS * TAIL] = packed[j * GR:(j + 1) * GR]
+                    head[k, z, g * NJ + j, :, 0:SLOTS * TAIL] = packed[j * GR:(j + 1) * GR]
         ri = lax.broadcasted_iota(jnp.int32, (R, KP), 0) + o * R
         ci = lax.broadcasted_iota(jnp.int32, (R, KP), 1)
         mask = ri == ci
@@ -101,102 +215,49 @@
             dq = jnp.sum(jnp.where(mask, oloc[q, :, 0:KP], 0.0), axis=0, keepdims=True)
             tq = jnp.sum(dq, axis=1, keepdims=True)
             tr = tr + jnp.where(lane == q, jnp.broadcast_to(tq, (GR, LANES)), 0.0)
-        tails[o, GROUPS * NJ] = tr
+        head[k, z, HT] = tr
+        for q in range(Q):
+            repack(q)
 
         pl.semaphore_wait(bar, has_r.astype(jnp.int32) + has_l.astype(jnp.int32) + W)
-
-        def piece(d, u):
-            if isinstance(u, str):
-                return {"a": amps, "t": tails}[u].at[d], {"a": Q, "t": Q + 1}[u]
-            return gath.at[d, pl.ds(u * NJ, NJ)], u
-
-        def remote(d, u, sems, target):
-            ref, i = piece(d, u)
-            return pltpu.make_async_remote_copy(
-                src_ref=ref, dst_ref=ref, send_sem=sems.at[d, i], recv_sem=r_sem.at[d, i],
-                device_id=(v, target), device_id_type=MESH)
-
-        def send_own(u):
-            @pl.when(has_r)
-            def _():
-                remote(o, u, s_right, right).start()
-
-            @pl.when(has_l)
-            def _():
-                remote(o, u, s_left, left).start()
-
-            remote(o, u, s_part, part).start()
-
-        def relay(h, u):
-            @pl.when(z - h >= 0)
-            def _():
-                d = (z - h) * CORES + k
-                remote(d, u, s_right, right).wait_recv()
-
-                @pl.when(has_r)
-                def _():
-                    remote(d, u, s_right, right).start()
-
-                remote(d, u, s_part, part).start()
-
-            @pl.when(z + h < NZ)
-            def _():
-                d = (z + h) * CORES + k
-                remote(d, u, s_left, left).wait_recv()
-
-                @pl.when(has_l)
-                def _():
-                    remote(d, u, s_left, left).start()
-
-                remote(d, u, s_part, part).start()
-
-        def from_partner(u):
-            for s in range(NZ):
-                remote(s * CORES + 1 - k, u, s_part, part).wait_recv()
-
-        units = ["a", "t"] + list(range(Q))
-        LEAD = 2 + SKEW * max(NZ - 2, 0)
-
-        def finish(u):
-            for s in range(NZ):
-                d = s * CORES + k
-
-                @pl.when(jnp.logical_and(s <= z, has_r))
-                def _():
-                    remote(d, u, s_right, right).wait_send()
-
-                @pl.when(jnp.logical_and(s >= z, has_l))
-                def _():
-                    remote(d, u, s_left, left).wait_send()
-
-                remote(d, u, s_part, part).wait_send()
 
         for u in units[:AHEAD]:
             send_own(u)
-
-        @pl.loop(0, Q)
-        def _(q):
-            vin(q).start()
+        c_vir.start()
 
         for q in range(Q):
             for r in range(R):
                 drows[r * Q + q:r * Q + q + 1, :] = oloc[q, r:r + 1, :]
 
-        for t in range(LEAD):
+        for t in range(START):
             if AHEAD <= t + AHEAD < UNITS:
                 send_own(units[t + AHEAD])
             for h in range(1, NZ):
                 n = t - SKEW * (h - 1)
                 if 0 <= n < UNITS:
                     relay(h, units[n])
-        from_partner("a")
-        from_partner("t")
+            if t == LAG:
+                from_partner("h")
+
+                @pl.when(v < NCH)
+                def _():
+                    for h in range(1, W):
+                        a_copy(h).start()
+
+        for c in range(NCH):
+            a_wait(c)
+
+            @pl.when(c == v)
+            def _():
+                amps[c] = head[:, :, HS:HS + NJ * CH]
 
         xbuf[...] = jnp.zeros_like(xbuf)
         for d in range(D):
             for j in range(NJ):
                 at = d * R + j * GR
-                xbuf[at:at + GR, 0:A] = amps[d, j]
+                for t in range(TILES):
+                    xbuf[at:at + GR, t * LANES:(t + 1) * LANES] = (
+                        amps[t // CH, d % CORES, d // CORES, j * CH + t % CH])
         amp = xbuf[0:OCC, 0:A]
         tmat[...] = jnp.zeros_like(tmat)
         shifted = jnp.concatenate([jnp.zeros((OCC, OCC), F32), amp], axis=1)
@@ -225,9 +286,9 @@
             sl = drows[:, OCC + w * PIECE:OCC + (w + 1) * PIECE]
             for r in range(R):
                 ovsend[w, r] = sl[r * Q:(r + 1) * Q]
-        total = tails[0, GROUPS * NJ]
+        total = head[0, 0, HT]
         for d in range(1, D):
-            total = total + tails[d, GROUPS * NJ]
+            total = total + head[d % CORES, d // CORES, HT]
         rid = lax.broadcasted_iota(jnp.int32, (R, ROWS), 0) * Q
         cid = lax.broadcasted_iota(jnp.int32, (R, ROWS), 1)
         wts = jnp.zeros((R, ROWS), F32)
@@ -256,33 +317,22 @@
             f_copy(h).start()
         ovrecv[v] = ovsend[v]
 
-        @pl.loop(0, Q)
-        def _(q):
-            @pl.when(q + LEAD + AHEAD < UNITS)
-            def _():
-                send_own(q + LEAD + AHEAD - 2)
-
-            for h in range(1, NZ):
-                n = q + LEAD - SKEW * (h - 1)
-
-                @pl.when(n < UNITS)
-                def _():
-                    relay(h, n - 2)
-
+        c_vir.wait()
+
+        def dress(q):
             from_partner(q)
             if TAIL:
                 shift = lax.rem(LANES - lax.rem(q, SLOTS) * TAIL, LANES)
             for d in range(D):
                 for j in range(NJ):
                     at = d * R + j * GR
-                    xbuf[at:at + GR, 0:MAIN] = gath[d, q * NJ + j]
+                    xbuf[at:at + GR, 0:MAIN] = gath[d % CORES, d // CORES, q * NJ + j]
                     if TAIL:
-                        t = pltpu.roll(tails[d, (q // SLOTS) * NJ + j], shift, axis=1)
+                        t = pltpu.roll(head[d % CORES, d // CORES, (q // SLOTS) * NJ + j], shift, axis=1)
                         xbuf[at:at + GR, MAIN:N] = t[:, 0:TAIL]
             hi, lo = split(jnp.transpose(xbuf[...])[0:N])
             prod = dot(jnp.concatenate([hi, lo], axis=1), sleft[...])
             prod = prod[:, 0:VP] + prod[:, VP:2 * VP]
-            vin(q).wait()
             vloc[q] = vloc[q] - prod[:, 0:RV]
             hi, lo = split(vloc[q, 0:OCC, :])
             lwts[0:OCC, 0:RV] = hi
@@ -292,6 +342,28 @@
             prod = prod[:, 0:VP] + prod[:, VP:2 * VP]
             vloc[q, OCC:N, :] = vloc[q, OCC:N, :] + prod[:, 0:RV]
             vout(q).start()
+
+        def done(t):
+            return jnp.minimum(t - LAG, RATE * (t - START + 1))
+
+        @pl.loop(START, STEPS)
+        def _(t):
+            @pl.when(t + AHEAD < UNITS)
+            def _():
+                send_own(t + AHEAD - 1)
+
+            for h in range(1, NZ):
+                n = t - SKEW * (h - 1)
+
+                @pl.when(n < UNITS)
+                def _():
+                    relay(h, n - 1)
+
+            lo = jnp.where(t == START, 0, done(t - 1))
+
+            @pl.loop(lo, done(t))
+            def _(q):
+                dress(q)
 
         for h in range(1, W):
             ov_copy(h).wait_recv()
@@ -309,13 +381,13 @@
         c_f = pltpu.make_async_copy(fout, out_fock, o_out.at[1])
         c_f.start()
 
-        finish("a")
-        finish("t")
-
-        @pl.loop(0, Q)
-        def _(u):
-            finish(u)
-            vout(u).wait()
+        finish()
+        pltpu.make_async_copy(vloc, out_vir, v_out.at[0]).wait()
+
+        @pl.when(v < NCH)
+        def _():
+            for h in range(1, W):
+                a_copy(h).wait_send()
 
         for h in range(1, W):
             ov_copy(h).wait_send()
@@ -335,9 +407,9 @@
         in_specs=[pl.BlockSpec(memory_space=pltpu.HBM)] * 3,
         out_specs=(any_spec,) * 3,
         scratch_shapes=[
-            V((D, GRAN, GR, MAIN), F32),
-            V((D, NJ, GR, A), F32),
-            V((D, GROUPS * NJ + 1, GR, LANES), F32),
+            V((CORES, NZ, GRAN, GR, MAIN), F32),
+            V((CORES, NZ, HEAD, GR, LANES), F32),
+            V((NCH, CORES, NZ, NJ * CH, GR, LANES), F32),
             V((Q, N, RV), F32),
             V((Q, R, N), F32),
             V((R, A), F32),
@@ -352,9 +424,9 @@
             V((R, Q * W, PIECE), F32),
             V((W, NJ, GR, A), F32),
             V((R, A), F32),
-            DMA((D, UNITS)), DMA((D, UNITS)), DMA((D, UNITS)), DMA((D, UNITS)),
-            DMA((W,)), DMA((W,)), DMA((W,)), DMA((W,)),
-            DMA((2,)), DMA((Q,)), DMA((Q,)), DMA((2,)),
+            DMA((NZ, 2)), DMA((NZ, 2)), DMA((NZ, 2)), DMA((NZ, UNITS)), DMA((UNITS,)),
+            DMA((W,)), DMA((NCH,)), DMA((W,)), DMA((W,)), DMA((W,)), DMA((W,)),
+            DMA((2,)), DMA((1,)), DMA((1,)), DMA((2,)),
         ],
         compiler_params=pltpu.CompilerParams(
             collective_id=0, has_side_effects=True, vmem_limit_bytes=40 * 2**20),

time: 57.7 us -> 51.6 us (0.89)
  Pallas kernels: 56.9 us -> 50.8 us
    pallas_call x1, Pallas kernels: 54.1 us -> 48 us  [shards(): call(*(pltpu.with_memory_space_constraint(a, pltpu.HBM) for a in args))]
where the time goes in v1:
time: 51.6 us; the launch traced here: 51.4 us
  Pallas kernels  50.8 us (98%)
  between operations  0.64 us (1%)
    pallas_call x1, Pallas kernels, shards(): call(*(pltpu.with_memory_space_constraint(a, pltpu.HBM) for a in args))  48 us
    pallas_call x1, Pallas kernels, store(): pl.pallas_call(write_out, name='store', out_shape=tuple((jax.ShapeDtypeSt...  2.8 us

profile of v1, /device:TPU:0, one launch (start us, length us, event | category | flops | bytes accessed | tf_op | source)
XLA Modules:
  0.0 51.4 jit_solution(15958349610695764993)
XLA Ops:
  0.6 48.0 %dress.1 = (f32[11,1056,120]{2,1,0:T(8,128)S(1)}, f32[12,44,240]{2,1,0:T(8,128)S(1)}, f32[12,960]{1,0:T(8,128)S(1)}) custom-call(f32[11,12,1056]{2,1,0:T(8,128)} %occ.1, f32[11,1056,120]{2,1,0:T(8,128)} %bitcast.3, f32[12,960]{1,0:T(8,128)} %sing.1), custom_call_target="tpu_custom_call" | custom-call | tf_op jit(solution)/shard_map/dress/pallas_call | solution.py:464
  48.6 2.8 %store.1 = (f32[11,1056,120]{2,1,0:T(8,128)}, f32[12,44,240]{2,1,0:T(8,128)}, f32[12,960]{1,0:T(8,128)}) custom-call(f32[11,1056,120]{2,1,0:T(8,128)S(1)} %get-tuple-element.9.refs_0_, f32[12,44,240]{2,1,0:T(8,128)S(1)} %get-tuple-element.10.refs_1_, f32[12,960]{1,0:T(8,128)S(1)} %get-tuple-element.11.refs_2_), custom_call_target="tpu_custom_call" | custom-call | tf_op jit(solution)/shard_map/store/pallas_call | solution.py:446

commit v2 on v1

--- a/solution.py
+++ b/solution.py
@@ -10,7 +10,7 @@
 LANES = 128
 CORES = 2
 SKEW = 1
-AHEAD = 4
+AHEAD = 8
 FIRST = 5
 RATE = 2
 
@@ -344,7 +344,7 @@
             vout(q).start()
 
         def done(t):
-            return jnp.minimum(t - LAG, RATE * (t - START + 1))
+            return jnp.where(t == STEPS - 1, Q, jnp.minimum(t - LAG - 1, RATE * (t - START + 1)))
 
         @pl.loop(START, STEPS)
         def _(t):

time: 51.6 us -> 49.9 us (0.967)
  Pallas kernels: 50.8 us -> 49.1 us
    pallas_call x1, Pallas kernels: 48 us -> 46.3 us  [shards(): call(*(pltpu.with_memory_space_constraint(a, pltpu.HBM) for a in args))]
where the time goes in v2:
time: 49.9 us; the launch traced here: 49.7 us
  Pallas kernels  49.1 us (98%)
  between operations  0.64 us (1%)
    pallas_call x1, Pallas kernels, shards(): call(*(pltpu.with_memory_space_constraint(a, pltpu.HBM) for a in args))  46.3 us
    pallas_call x1, Pallas kernels, store(): pl.pallas_call(write_out, name='store', out_shape=tuple((jax.ShapeDtypeSt...  2.8 us

profile of v2, /device:TPU:0, one launch (start us, length us, event | category | flops | bytes accessed | tf_op | source)
XLA Modules:
  0.0 49.7 jit_solution(967759184182347539)
XLA Ops:
  0.6 46.3 %dress.1 = (f32[11,1056,120]{2,1,0:T(8,128)S(1)}, f32[12,44,240]{2,1,0:T(8,128)S(1)}, f32[12,960]{1,0:T(8,128)S(1)}) custom-call(f32[11,12,1056]{2,1,0:T(8,128)} %occ.1, f32[11,1056,120]{2,1,0:T(8,128)} %bitcast.3, f32[12,960]{1,0:T(8,128)} %sing.1), custom_call_target="tpu_custom_call" | custom-call | tf_op jit(solution)/shard_map/dress/pallas_call | solution.py:464
  46.9 2.8 %store.1 = (f32[11,1056,120]{2,1,0:T(8,128)}, f32[12,44,240]{2,1,0:T(8,128)}, f32[12,960]{1,0:T(8,128)}) custom-call(f32[11,1056,120]{2,1,0:T(8,128)S(1)} %get-tuple-element.9.refs_0_, f32[12,44,240]{2,1,0:T(8,128)S(1)} %get-tuple-element.10.refs_1_, f32[12,960]{1,0:T(8,128)S(1)} %get-tuple-element.11.refs_2_), custom_call_target="tpu_custom_call" | custom-call | tf_op jit(solution)/shard_map/store/pallas_call | solution.py:446

commit v3 on v2

--- a/solution.py
+++ b/solution.py
@@ -10,7 +10,7 @@
 LANES = 128
 CORES = 2
 SKEW = 1
-AHEAD = 8
+AHEAD = 5
 FIRST = 5
 RATE = 2
 
@@ -55,7 +55,7 @@
                gath, head, amps, vloc, oloc, sloc, xbuf, drows, tmat, tright, sleft, lwts,
                ovsend, ovrecv, ovout, fbuf, fout,
                s_right, s_left, s_part, r_dir, r_part, a_s, a_r, ov_s, ov_r, f_s, f_r,
-               in_sem, v_in, v_out, o_out):
+               in_sem, v_in, v_out, o_out, ready):
         v = lax.axis_index("vec")
         o = lax.axis_index("orb")
         z = o // CORES
@@ -82,13 +82,23 @@
         def _():
             pl.semaphore_signal(bar, inc=1, device_id=(v, right), device_id_type=MESH)
 
+        pl.semaphore_signal(bar, inc=1, device_id=(v, part), device_id_type=MESH)
+        for h in range(1, W):
+            @pl.when(v + h < W)
+            def _():
+                pl.semaphore_signal(bar, inc=1, device_id=(lax.rem(v + h, W), o), device_id_type=MESH)
+
+        pl.semaphore_wait(bar, has_l.astype(jnp.int32) + v + 1)
+
         @pl.when(has_l)
         def _():
-            pl.semaphore_signal(bar, inc=1, device_id=(v, left), device_id_type=MESH)
-
-        pl.semaphore_signal(bar, inc=1, device_id=(v, part), device_id_type=MESH)
+            pl.semaphore_signal(ready.at[0], inc=1, device_id=(v, left), device_id_type=MESH)
+
         for h in range(1, W):
-            pl.semaphore_signal(bar, inc=1, device_id=(lax.rem(v + h, W), o), device_id_type=MESH)
+            @pl.when(v - h >= 0)
+            def _():
+                pl.semaphore_signal(ready.at[1], inc=1, device_id=(lax.rem(v - h + W, W), o),
+                                    device_id_type=MESH)
 
         def piece(c, s, u):
             if isinstance(u, str):
@@ -107,16 +117,21 @@
                 src_ref=ref, dst_ref=ref, send_sem=s_part.at[s, kind], recv_sem=r_part.at[i],
                 device_id=(v, part), device_id_type=MESH)
 
+        def send_left(u):
+            @pl.when(has_l)
+            def _():
+                remote(z, u, s_left, left).start()
+
+            across(z, u).start()
+
+        def send_right(u):
+            @pl.when(has_r)
+            def _():
+                remote(z, u, s_right, right).start()
+
         def send_own(u):
-            @pl.when(has_r)
-            def _():
-                remote(z, u, s_right, right).start()
-
-            @pl.when(has_l)
-            def _():
-                remote(z, u, s_left, left).start()
-
-            across(z, u).start()
+            send_left(u)
+            send_right(u)
 
         def relay(h, u):
             @pl.when(z - h >= 0)
@@ -188,6 +203,8 @@
 
         units = ["h"] + list(range(Q))
         c_occ.wait()
+        repack(0)
+        send_left(0)
         c_sing.wait()
         full = sloc[...]
         if NCH * CH * LANES > A:
@@ -216,13 +233,19 @@
             tq = jnp.sum(dq, axis=1, keepdims=True)
             tr = tr + jnp.where(lane == q, jnp.broadcast_to(tq, (GR, LANES)), 0.0)
         head[k, z, HT] = tr
-        for q in range(Q):
+        for q in range(1, Q):
             repack(q)
 
-        pl.semaphore_wait(bar, has_r.astype(jnp.int32) + has_l.astype(jnp.int32) + W)
-
         for u in units[:AHEAD]:
-            send_own(u)
+            if u != 0:
+                send_left(u)
+
+        @pl.when(has_r)
+        def _():
+            pl.semaphore_wait(ready.at[0], 1)
+
+        for u in units[:AHEAD]:
+            send_right(u)
         c_vir.start()
 
         for q in range(Q):
@@ -238,6 +261,10 @@
                     relay(h, units[n])
             if t == LAG:
                 from_partner("h")
+
+                @pl.when(v < W - 1)
+                def _():
+                    pl.semaphore_wait(ready.at[1], W - 1 - v)
 
                 @pl.when(v < NCH)
                 def _():
@@ -426,7 +453,7 @@
             V((R, A), F32),
             DMA((NZ, 2)), DMA((NZ, 2)), DMA((NZ, 2)), DMA((NZ, UNITS)), DMA((UNITS,)),
             DMA((W,)), DMA((NCH,)), DMA((W,)), DMA((W,)), DMA((W,)), DMA((W,)),
-            DMA((2,)), DMA((1,)), DMA((1,)), DMA((2,)),
+            DMA((2,)), DMA((1,)), DMA((1,)), DMA((2,)), pltpu.SemaphoreType.REGULAR((2,)),
         ],
         compiler_params=pltpu.CompilerParams(
             collective_id=0, has_side_effects=True, vmem_limit_bytes=40 * 2**20),

time: 49.9 us -> 48.9 us (0.980)
  Pallas kernels: 49.1 us -> 48.1 us
    pallas_call x1, Pallas kernels: 46.3 us -> 45.3 us  [shards(): call(*(pltpu.with_memory_space_constraint(a, pltpu.HBM) for a in args))]
where the time goes in v3:
time: 48.9 us; the launch traced here: 48.7 us
  Pallas kernels  48.1 us (98%)
  between operations  0.64 us (1%)
    pallas_call x1, Pallas kernels, shards(): call(*(pltpu.with_memory_space_constraint(a, pltpu.HBM) for a in args))  45.3 us
    pallas_call x1, Pallas kernels, store(): pl.pallas_call(write_out, name='store', out_shape=tuple((jax.ShapeDtypeSt...  2.8 us

profile of v3, /device:TPU:0, one launch (start us, length us, event | category | flops | bytes accessed | tf_op | source)
XLA Modules:
  0.0 48.7 jit_solution(9900053529045908959)
XLA Ops:
  0.6 45.3 %dress.1 = (f32[11,1056,120]{2,1,0:T(8,128)S(1)}, f32[12,44,240]{2,1,0:T(8,128)S(1)}, f32[12,960]{1,0:T(8,128)S(1)}) custom-call(f32[11,12,1056]{2,1,0:T(8,128)} %occ.1, f32[11,1056,120]{2,1,0:T(8,128)} %bitcast.3, f32[12,960]{1,0:T(8,128)} %sing.1), custom_call_target="tpu_custom_call" | custom-call | tf_op jit(solution)/shard_map/dress/pallas_call | solution.py:491
  45.9 2.8 %store.1 = (f32[11,1056,120]{2,1,0:T(8,128)}, f32[12,44,240]{2,1,0:T(8,128)}, f32[12,960]{1,0:T(8,128)}) custom-call(f32[11,1056,120]{2,1,0:T(8,128)S(1)} %get-tuple-element.9.refs_0_, f32[12,44,240]{2,1,0:T(8,128)S(1)} %get-tuple-element.10.refs_1_, f32[12,960]{1,0:T(8,128)S(1)} %get-tuple-element.11.refs_2_), custom_call_target="tpu_custom_call" | custom-call | tf_op jit(solution)/shard_map/store/pallas_call | solution.py:473

commit v4 on v3

--- a/solution.py
+++ b/solution.py
@@ -50,12 +50,13 @@
     LAG = SKEW * max(NZ - 2, 0)
     STEPS = UNITS + LAG
     START = max(FIRST, LAG + 1)
-
-    def kernel(occ, vir, sing, out_vir, out_ov, out_fock,
-               gath, head, amps, vloc, oloc, sloc, xbuf, drows, tmat, tright, sleft, lwts,
-               ovsend, ovrecv, ovout, fbuf, fout,
+    GATHER = max(START, STEPS - 4)
+
+    def kernel(occ, vir, sing, vloc, ovout, fout,
+               gath, head, amps, oloc, sloc, xbuf, drows, tmat, tright, sleft, lwts,
+               ovsend, ovrecv, fbuf,
                s_right, s_left, s_part, r_dir, r_part, a_s, a_r, ov_s, ov_r, f_s, f_r,
-               in_sem, v_in, v_out, o_out, ready):
+               in_sem, v_in, ready):
         v = lax.axis_index("vec")
         o = lax.axis_index("orb")
         z = o // CORES
@@ -73,9 +74,6 @@
 
         c_vir = pltpu.make_async_copy(vir, vloc, v_in.at[0])
 
-        def vout(q):
-            return pltpu.make_async_copy(vloc.at[q], out_vir.at[q], v_out.at[0])
-
         bar = pltpu.get_barrier_semaphore()
 
         @pl.when(has_r)
@@ -108,13 +106,13 @@
         def remote(s, u, sems, target):
             ref, i, kind = piece(k, s, u)
             return pltpu.make_async_remote_copy(
-                src_ref=ref, dst_ref=ref, send_sem=sems.at[s, kind], recv_sem=r_dir.at[s, i],
+                src_ref=ref, dst_ref=ref, send_sem=sems.at[kind], recv_sem=r_dir.at[s, i],
                 device_id=(v, target), device_id_type=MESH)
 
         def across(s, u):
             ref, i, kind = piece(k, s, u)
             return pltpu.make_async_remote_copy(
-                src_ref=ref, dst_ref=ref, send_sem=s_part.at[s, kind], recv_sem=r_part.at[i],
+                src_ref=ref, dst_ref=ref, send_sem=s_part.at[kind], recv_sem=r_part.at[i],
                 device_id=(v, part), device_id_type=MESH)
 
         def send_left(u):
@@ -162,26 +160,25 @@
             else:
                 ref, i = gath.at[1 - k, :, pl.ds(u * NJ, NJ)], u + 1
             pltpu.make_async_remote_copy(
-                src_ref=ref, dst_ref=ref, send_sem=s_part.at[0, 0], recv_sem=r_part.at[i],
+                src_ref=ref, dst_ref=ref, send_sem=s_part.at[0], recv_sem=r_part.at[i],
                 device_id=(v, part), device_id_type=MESH).wait_recv()
 
         def finish():
-            for s in range(NZ):
-                for kind, ref in enumerate((head.at[k, s], gath.at[k, s])):
-                    def drain(sems, target):
-                        pltpu.make_async_remote_copy(
-                            src_ref=ref, dst_ref=ref, send_sem=sems.at[s, kind], recv_sem=r_dir.at[s, 0],
-                            device_id=(v, target), device_id_type=MESH).wait_send()
-
-                    @pl.when(jnp.logical_and(s <= z, has_r))
+            for kind, ref in enumerate((head, gath)):
+                def drain(lo, hi, sems, target):
+                    sent = ref.at[k, lo:hi]
+                    pltpu.make_async_remote_copy(
+                        src_ref=sent, dst_ref=sent, send_sem=sems.at[kind], recv_sem=r_dir.at[0, 0],
+                        device_id=(v, target), device_id_type=MESH).wait_send()
+
+                drain(0, NZ, s_part, part)
+                for i in range(NZ):
+                    @pl.when(z == i)
                     def _():
-                        drain(s_right, right)
-
-                    @pl.when(jnp.logical_and(s >= z, has_l))
-                    def _():
-                        drain(s_left, left)
-
-                    drain(s_part, part)
+                        if i < NZ - 1:
+                            drain(0, i + 1, s_right, right)
+                        if i > 0:
+                            drain(i, NZ, s_left, left)
 
         def a_copy(h):
             w = lax.rem(v + h, W)
@@ -368,7 +365,19 @@
             prod = dot(tright[...], lwts[...])
             prod = prod[:, 0:VP] + prod[:, VP:2 * VP]
             vloc[q, OCC:N, :] = vloc[q, OCC:N, :] + prod[:, 0:RV]
-            vout(q).start()
+
+        def collect():
+            for h in range(1, W):
+                ov_copy(h).wait_recv()
+                f_copy(h).wait_recv()
+            for w in range(W):
+                for r in range(R):
+                    ovout[r, w * Q:(w + 1) * Q, :] = ovrecv[w, r]
+            for j in range(NJ):
+                acc = fbuf[0, j]
+                for w in range(1, W):
+                    acc = acc + fbuf[w, j]
+                fout[j * GR:(j + 1) * GR, :] = acc / (Q * W)
 
         def done(t):
             return jnp.where(t == STEPS - 1, Q, jnp.minimum(t - LAG - 1, RATE * (t - START + 1)))
@@ -392,24 +401,11 @@
             def _(q):
                 dress(q)
 
-        for h in range(1, W):
-            ov_copy(h).wait_recv()
-            f_copy(h).wait_recv()
-        for w in range(W):
-            for r in range(R):
-                ovout[r, w * Q:(w + 1) * Q, :] = ovrecv[w, r]
-        c_ov = pltpu.make_async_copy(ovout, out_ov, o_out.at[0])
-        c_ov.start()
-        for j in range(NJ):
-            acc = fbuf[0, j]
-            for w in range(1, W):
-                acc = acc + fbuf[w, j]
-            fout[j * GR:(j + 1) * GR, :] = acc / (Q * W)
-        c_f = pltpu.make_async_copy(fout, out_fock, o_out.at[1])
-        c_f.start()
+            @pl.when(t == GATHER)
+            def _():
+                collect()
 
         finish()
-        pltpu.make_async_copy(vloc, out_vir, v_out.at[0]).wait()
 
         @pl.when(v < NCH)
         def _():
@@ -419,12 +415,9 @@
         for h in range(1, W):
             ov_copy(h).wait_send()
             f_copy(h).wait_send()
-        c_ov.wait()
-        c_f.wait()
 
     DMA = pltpu.SemaphoreType.DMA
     V = pltpu.VMEM
-    any_spec = pl.BlockSpec(memory_space=pl.ANY)
     return pl.pallas_call(
         kernel,
         name="dress",
@@ -432,12 +425,11 @@
                    jax.ShapeDtypeStruct((R, Q * W, PIECE), F32),
                    jax.ShapeDtypeStruct((R, A), F32)),
         in_specs=[pl.BlockSpec(memory_space=pltpu.HBM)] * 3,
-        out_specs=(any_spec,) * 3,
+        out_specs=(pl.BlockSpec(memory_space=pltpu.VMEM),) * 3,
         scratch_shapes=[
             V((CORES, NZ, GRAN, GR, MAIN), F32),
             V((CORES, NZ, HEAD, GR, LANES), F32),
             V((NCH, CORES, NZ, NJ * CH, GR, LANES), F32),
-            V((Q, N, RV), F32),
             V((Q, R, N), F32),
             V((R, A), F32),
             V((KP, NP), F32),
@@ -448,12 +440,10 @@
             V((2 * KP, 2 * VP), BF16),
             V((W, R, Q, PIECE), F32),
             V((W, R, Q, PIECE), F32),
-            V((R, Q * W, PIECE), F32),
             V((W, NJ, GR, A), F32),
-            V((R, A), F32),
-            DMA((NZ, 2)), DMA((NZ, 2)), DMA((NZ, 2)), DMA((NZ, UNITS)), DMA((UNITS,)),
+            DMA((2,)), DMA((2,)), DMA((2,)), DMA((NZ, UNITS)), DMA((UNITS,)),
             DMA((W,)), DMA((NCH,)), DMA((W,)), DMA((W,)), DMA((W,)), DMA((W,)),
-            DMA((2,)), DMA((1,)), DMA((1,)), DMA((2,)), pltpu.SemaphoreType.REGULAR((2,)),
+            DMA((2,)), DMA((1,)), pltpu.SemaphoreType.REGULAR((2,)),
         ],
         compiler_params=pltpu.CompilerParams(
             collective_id=0, has_side_effects=True, vmem_limit_bytes=40 * 2**20),

time: 48.9 us -> 48.2 us (0.986)
  Pallas kernels: 48.1 us -> 47.4 us
    pallas_call x1, Pallas kernels: 45.3 us -> 44.6 us  [shards(): call(*(pltpu.with_memory_space_constraint(a, pltpu.HBM) for a in args))]
where the time goes in v4:
time: 48.2 us; the launch traced here: 48 us
  Pallas kernels  47.4 us (98%)
  between operations  0.64 us (1%)
    pallas_call x1, Pallas kernels, shards(): call(*(pltpu.with_memory_space_constraint(a, pltpu.HBM) for a in args))  44.6 us
    pallas_call x1, Pallas kernels, store(): pl.pallas_call(write_out, name='store', out_shape=tuple((jax.ShapeDtypeSt...  2.8 us

profile of v4, /device:TPU:0, one launch (start us, length us, event | category | flops | bytes accessed | tf_op | source)
XLA Modules:
  0.0 48.0 jit_solution(4582176966939414841)
XLA Ops:
  0.6 44.6 %dress.1 = (f32[11,1056,120]{2,1,0:T(8,128)S(1)}, f32[12,44,240]{2,1,0:T(8,128)S(1)}, f32[12,960]{1,0:T(8,128)S(1)}) custom-call(f32[11,12,1056]{2,1,0:T(8,128)} %occ.1, f32[11,1056,120]{2,1,0:T(8,128)} %bitcast.3, f32[12,960]{1,0:T(8,128)} %sing.1), custom_call_target="tpu_custom_call" | custom-call | tf_op jit(solution)/shard_map/dress/pallas_call | solution.py:481
  45.2 2.8 %store.1 = (f32[11,1056,120]{2,1,0:T(8,128)}, f32[12,44,240]{2,1,0:T(8,128)}, f32[12,960]{1,0:T(8,128)}) custom-call(f32[11,1056,120]{2,1,0:T(8,128)S(1)} %get-tuple-element.9.refs_0_, f32[12,44,240]{2,1,0:T(8,128)S(1)} %get-tuple-element.10.refs_1_, f32[12,960]{1,0:T(8,128)S(1)} %get-tuple-element.11.refs_2_), custom_call_target="tpu_custom_call" | custom-call | tf_op jit(solution)/shard_map/store/pallas_call | solution.py:463
